TPU v7x, 32 devices: a whole 2x2x4 slice. The times are simulated.
32 devices in a mesh: gx: 8 (over y, x, core), gy: 4 (over z).
Axes of the slice: x: 2, y: 2, z: 4, core: 2. Of those that a mesh axis runs over, the one named last changes fastest.
Arguments:
- thinker_normed: bfloat16 [4, 16, 8192], P(None, None, 'gx'), may hold values from -6 to 6
- thinker_resid: bfloat16 [4, 16, 8192], P('gy', None, 'gx'), may hold values from -6 to 6
- gate_weight: bfloat16 [8192, 29568], P('gx', 'gy'), may hold values from -0.0625 to 0.0625
- up_weight: bfloat16 [8192, 29568], P('gx', 'gy'), may hold values from -0.0625 to 0.0625
- down_weight: bfloat16 [29568, 8192], P('gy', 'gx'), may hold values from -0.03125 to 0.03125
- bridge_weight: bfloat16 [8192, 3584], P('gx'), may hold values from -0.0625 to 0.0625
- talker_stream: bfloat16 [4, 1536, 3584], P('gy', 'gx'), may hold values from -6 to 6
- norm_gain: float32 [3584], replicated, may hold values from 0.5 to 2
- w_query: bfloat16 [3584, 1792], P(None, 'gy'), may hold values from -0.09375 to 0.09375
- w_key: bfloat16 [3584, 256], P(None, 'gy'), may hold values from -0.09375 to 0.09375
- w_value: bfloat16 [3584, 256], P(None, 'gy'), may hold values from -0.09375 to 0.09375
- a_query: bfloat16 [3584, 64], replicated, may hold values from -0.09375 to 0.09375
- b_query: bfloat16 [64, 1792], replicated, may hold values from -0.75 to 0.75
- a_value: bfloat16 [3584, 64], replicated, may hold values from -0.09375 to 0.09375
- b_value: bfloat16 [64, 256], replicated, may hold values from -0.75 to 0.75
- text_index: int32 [4, 1536], P('gy', 'gx'), may hold values from 0 to 15
- span_offset: int32 [4], P('gy'), may hold values from 1 to 1535
- out_grad: bfloat16 [4, 1536, 1792], P('gy', 'gx'), may hold values from -6 to 6
Outputs:
- attn_out: bfloat16 [4, 1536, 1792], P('gy', 'gx')
- grad_aq: float32 [3584, 64], replicated
- grad_bq: float32 [64, 1792], replicated
- grad_av: float32 [3584, 64], replicated
- grad_bv: float32 [64, 256], replicated
All inputs are finite; a program needn't handle non-finite values.
Results may differ from a plain program's by a relative error of at most 0.035.
Values may be sent and summed in bfloat16 or wider, within the bound.
No kernel may reach another device: no remote copies, remote signals or barrier semaphores. Data moves between devices by JAX's collectives and lax.ppermute only.
A program may use at most 192 MiB of HBM per device.

v0:
```python
import math
import jax
import jax.numpy as jnp
from jax import lax
from jax.sharding import PartitionSpec as P

HEADS = 14
KVH = 2
HD = 128
rope_base = 1000000.0
norm_eps = 1e-06


def angle_tables(first_pos, length):
    position = (first_pos + jnp.arange(length, dtype=jnp.int32)).astype(jnp.float32)
    frequency = rope_base ** (-(2.0 * jnp.arange(HD // 2, dtype=jnp.float32)) / HD)
    angles = position[:, None] * frequency[None, :]
    return (jnp.cos(angles), jnp.sin(angles))


def rotate(tensor, cosine, sine_table, signed):
    layout = (cosine.shape[0],) + (1,) * (tensor.ndim - 2) + (cosine.shape[1],)
    cosine = cosine.reshape(layout)
    sine_part = sine_table.reshape(layout) * signed
    half_width = tensor.shape[-1] // 2
    first_half = tensor[..., :half_width]
    second_half = tensor[..., half_width:]
    return jnp.concatenate(
        [
            first_half * cosine - second_half * sine_part,
            second_half * cosine + first_half * sine_part,
        ],
        axis=-1,
    )


def on_device(
    thinker_normed,
    thinker_resid,
    gate_weight,
    up_weight,
    down_weight,
    bridge_weight,
    talker_stream,
    norm_gain,
    w_query,
    w_key,
    w_value,
    a_query,
    b_query,
    a_value,
    b_value,
    text_index,
    span_offset,
    out_grad,
):
    seq_count, rows_seq, columns = thinker_normed.shape
    normed = thinker_normed.reshape(seq_count * rows_seq, columns)
    ff_local = gate_weight.shape[1]
    block = normed
    gate_part = jnp.dot(block, gate_weight, preferred_element_type=jnp.float32)
    up_part = jnp.dot(block, up_weight, preferred_element_type=jnp.float32)
    both_parts = lax.psum_scatter(
        jnp.concatenate([gate_part, up_part], axis=1), "gx", scatter_dimension=0, tiled=True
    )
    hidden = (jax.nn.silu(both_parts[:, :ff_local]) * both_parts[:, ff_local:]).astype(jnp.bfloat16)
    partial_out = jnp.dot(
        lax.all_gather(hidden, "gx", axis=0, tiled=True),
        down_weight,
        preferred_element_type=jnp.float32,
    )
    summed = lax.psum_scatter(partial_out, "gy", scatter_dimension=0, tiled=True)
    thinker_out = (summed + thinker_resid[0].astype(jnp.float32)).astype(jnp.bfloat16)
    bridge_part = jnp.dot(thinker_out, bridge_weight, preferred_element_type=jnp.float32)
    bridge = lax.psum(bridge_part, "gx").astype(jnp.bfloat16)
    tokens = talker_stream.shape[1]
    groups = HEADS // KVH
    scale = 1.0 / math.sqrt(HD)
    picks = (text_index[0][:, None] == jnp.arange(rows_seq, dtype=jnp.int32)[None, :]).astype(
        jnp.bfloat16
    )
    mixed = talker_stream[0].astype(jnp.float32) + jnp.dot(
        picks, bridge, preferred_element_type=jnp.float32
    )
    normal = (
        mixed * lax.rsqrt(jnp.mean(mixed * mixed, axis=1, keepdims=True) + norm_eps) * norm_gain
    ).astype(jnp.bfloat16)
    low_query = jnp.dot(normal, a_query, preferred_element_type=jnp.float32).astype(jnp.bfloat16)
    low_value = jnp.dot(normal, a_value, preferred_element_type=jnp.float32).astype(jnp.bfloat16)
    slab_rows = lax.all_gather(normal, "gy", axis=0, tiled=True)
    projected = jnp.concatenate(
        [
            jnp.dot(slab_rows, w_query, preferred_element_type=jnp.float32),
            jnp.dot(slab_rows, w_key, preferred_element_type=jnp.float32),
            jnp.dot(slab_rows, w_value, preferred_element_type=jnp.float32),
        ],
        axis=1,
    )
    returned = lax.all_to_all(projected, "gy", split_axis=0, concat_axis=1, tiled=True)
    parcels = returned.reshape(tokens, lax.axis_size("gy"), -1)
    query_cols = w_query.shape[1]
    key_cols = w_key.shape[1]
    base_query = parcels[:, :, :query_cols].reshape(tokens, -1)
    base_key = parcels[:, :, query_cols : query_cols + key_cols].reshape(tokens, -1)
    base_value = parcels[:, :, query_cols + key_cols :].reshape(tokens, -1)
    first_pos = lax.axis_index("gx") * tokens
    cosine, sine_table = angle_tables(first_pos, tokens)
    query_pre = base_query + jnp.dot(low_query, b_query, preferred_element_type=jnp.float32)
    query = rotate(query_pre.reshape(tokens, KVH, groups, HD), cosine, sine_table, 1.0).astype(
        jnp.bfloat16
    )
    key_local = (
        rotate(base_key.reshape(tokens, KVH, HD), cosine, sine_table, 1.0)
        .astype(jnp.bfloat16)
        .reshape(tokens, KVH * HD)
    )
    value_local = (
        base_value + jnp.dot(low_value, b_value, preferred_element_type=jnp.float32)
    ).astype(jnp.bfloat16)
    key_all, value_all = (
        lax.all_gather(key_local, "gx", axis=0, tiled=True),
        lax.all_gather(value_local, "gx", axis=0, tiled=True),
    )
    length = key_all.shape[0]
    key_rows = key_all.reshape(length, KVH, HD)
    value_rows = value_all.reshape(length, KVH, HD)
    query_places = first_pos + jnp.arange(tokens, dtype=jnp.int32)
    key_places = jnp.arange(length, dtype=jnp.int32)
    causal = (key_places[None, :] <= query_places[:, None]) | (key_places[None, :] < span_offset[0])
    scores = (
        jnp.einsum("tkgd,skd->kgts", query, key_rows, preferred_element_type=jnp.float32) * scale
    )
    scores = jnp.where(causal, scores, -1e30)
    row_max = jnp.max(scores, axis=-1, keepdims=True)
    weights = jnp.exp(scores - row_max)
    probs = (weights / jnp.sum(weights, axis=-1, keepdims=True)).astype(jnp.bfloat16)
    attended = jnp.einsum(
        "kgts,skd->tkgd", probs, value_rows, preferred_element_type=jnp.float32
    ).astype(jnp.bfloat16)
    grad_four = out_grad[0].reshape(tokens, KVH, groups, HD)
    inner_prod = jnp.sum(grad_four.astype(jnp.float32) * attended.astype(jnp.float32), axis=-1)
    dprob = jnp.einsum("tkgd,skd->kgts", grad_four, value_rows, preferred_element_type=jnp.float32)
    dscore = (
        probs.astype(jnp.float32) * (dprob - jnp.transpose(inner_prod, (1, 2, 0))[..., None])
    ).astype(jnp.bfloat16)
    dquery = (
        jnp.einsum("kgts,skd->tkgd", dscore, key_rows, preferred_element_type=jnp.float32) * scale
    )
    query_grad = (
        rotate(dquery, cosine, sine_table, -1.0).reshape(tokens, HEADS * HD).astype(jnp.bfloat16)
    )
    block = probs
    term = jnp.einsum("kgts,tkgd->skd", block, grad_four, preferred_element_type=jnp.float32)
    value_grad = lax.psum_scatter(
        term.reshape(lax.axis_size("gx") * tokens, KVH * HD), "gx", scatter_dimension=0, tiled=True
    ).astype(jnp.bfloat16)
    part_bq = jnp.einsum("tr,tc->rc", low_query, query_grad, preferred_element_type=jnp.float32)
    part_bv = jnp.einsum("tr,tc->rc", low_value, value_grad, preferred_element_type=jnp.float32)
    dlow_query = jnp.einsum(
        "tc,rc->tr", query_grad, b_query, preferred_element_type=jnp.float32
    ).astype(jnp.bfloat16)
    dlow_value = jnp.einsum(
        "tc,rc->tr", value_grad, b_value, preferred_element_type=jnp.float32
    ).astype(jnp.bfloat16)
    part_aq = jnp.einsum("td,tr->dr", normal, dlow_query, preferred_element_type=jnp.float32)
    part_av = jnp.einsum("td,tr->dr", normal, dlow_value, preferred_element_type=jnp.float32)
    grad_aq, grad_bq, grad_av, grad_bv = lax.psum(
        (part_aq, part_bq, part_av, part_bv), ("gx", "gy")
    )
    attn_out = attended.reshape(1, tokens, HEADS * HD)
    return (attn_out, grad_aq, grad_bq, grad_av, grad_bv)


def solution(mesh):
    return jax.shard_map(
        on_device,
        mesh=mesh,
        in_specs=(
            P(None, None, "gx"),
            P("gy", None, "gx"),
            P("gx", "gy"),
            P("gx", "gy"),
            P("gy", "gx"),
            P("gx", None),
            P("gy", "gx", None),
            P(),
            P(None, "gy"),
            P(None, "gy"),
            P(None, "gy"),
            P(),
            P(),
            P(),
            P(),
            P("gy", "gx"),
            P("gy"),
            P("gy", "gx", None),
        ),
        out_specs=(P("gy", "gx", None), P(), P(), P(), P()),
        check_vma=False,
    )
```

profile of v0, /device:TPU:0, one launch (start us, length us, event | category | flops | bytes accessed | tf_op | source)
XLA Modules:
  0.0 564.3 jit_solution(9775176805287978987)
XLA Ops:
  7.2 10.2 %fusion.54 = f32[64,7392]{1,0:T(8,128)S(1)} fusion(bf16[64,1024]{1,0:T(8,128)(2,1)} %bitcast.100, bf16[1024,7392]{0,1:T(8,128)(2,1)} %param.20), kind=kOutput, calls=%fused_computation.78 | convolution fusion | flops 968884224 | bytes 17162240 | tf_op jit(solution)/shard_map/dot_general | solution.py:61
  17.4 10.0 %fusion.55 = f32[64,7392]{1,0:T(8,128)S(1)} fusion(bf16[64,1024]{1,0:T(8,128)(2,1)S(1)} %bitcast.101, bf16[1024,7392]{0,1:T(8,128)(2,1)} %param.21), kind=kOutput, calls=%fused_computation.79 | convolution fusion | flops 968884224 | bytes 17162240 | tf_op jit(solution)/shard_map/dot_general | solution.py:62
  27.4 2.5 pad_maximum_fusion
  29.9 52.0 %reduce-scatter.6.cloned.1.call-done = f32[8,14784]{1,0:T(8,128)} async-done(((f32[64,14784]{1,0:T(8,128)}), f32[8,14784]{1,0:T(8,128)}) %reduce-scatter.6.cloned.1.call-update) | async-done | bytes 473104 | tf_op jit(solution)/shard_map/reduce_scatter | solution.py:63
  81.9 1.2 fusion.32
  83.1 10.8 %all_gather.12 = bf16[64,7392]{1,0:T(8,128)(2,1)S(1)} all-gather(bf16[8,7392]{1,0:T(8,128)(2,1)S(1)} %fusion.32), channel_id=1, replica_groups=mesh['gx'=8,'gy'=4] {'gx'}, dimensions={0}, use_global_device_ids=true | all-gather | bytes 1064448 | tf_op jit(solution)/shard_map/all_gather | solution.py:68
  93.9 8.8 %fusion.56 = f32[64,1024]{1,0:T(8,128)} fusion(bf16[64,7392]{1,0:T(8,128)(2,1)S(1)} %all_gather.12, bf16[7392,1024]{1,0:T(8,128)(2,1)} %param.22), kind=kOutput, calls=%fused_computation.80 | convolution fusion | flops 968884224 | bytes 16347136 | tf_op jit(solution)/shard_map/dot_general | solution.py:67
  102.7 20.1 %reduce-scatter.8.cloned.1.call-done = f32[16,1024]{1,0:T(8,128)} async-done(((f32[64,1024]{1,0:T(8,128)}), f32[16,1024]{1,0:T(8,128)}) %reduce-scatter.8.cloned.1.call-update) | async-done | bytes 65552 | tf_op jit(solution)/shard_map/reduce_scatter | solution.py:72
  122.8 4.2 fusion.41
  127.0 25.4 %all-reduce.5 = bf16[16,3584]{1,0:T(8,128)(2,1)S(1)} all-reduce(f32[16,3584]{1,0:T(8,128)S(1)} %fusion.41), channel_id=1, replica_groups=mesh['gx'=8,'gy'=4] {'gx'}, use_global_device_ids=true, to_apply=%region_2.3 | all-reduce | flops 57344 | bytes 344064 | tf_op jit(solution)/shard_map/psum | solution.py:75
  152.4 2.0 multiply_reduce_fusion
  154.4 1.5 multiply_convert_fusion
  155.9 99.9 %all-gather.2.cloned.1.call-done = bf16[768,3584]{1,0:T(8,128)(2,1)} async-done(((bf16[192,3584]{1,0:T(8,128)(2,1)}), bf16[768,3584]{1,0:T(8,128)(2,1)}) %all-gather.2.cloned.1.call-update) | async-done | bytes 5505040 | tf_op jit(solution)/shard_map/all_gather | solution.py:90
  255.8 5.4 fusion.57
  261.2 1.8 fusion.58
  263.0 1.8 fusion.59
  264.9 1.8 copy.44
  266.7 4.6 all-to-all-start
  273.9 1.7 reshape_squeeze.3
  277.1 1.6 convolution_convert_fusion.4
  278.7 38.4 %all-to-all-done = f32[4,192,576]{2,1,0:T(8,128)} async-done(((f32[4,192,576]{2,1,0:T(8,128)}), f32[4,192,576]{2,1,0:T(8,128)}, u32[]{:S(2)}, u32[]{:S(2)}) %all-to-all-start) | async-done | bytes 1769504 | tf_op jit(solution)/shard_map/all_to_all | solution.py:99
  317.0 1.5 slice.50
  318.6 2.1 fusion.51
  320.7 2.2 copy.52
  322.8 2.5 reshape.208
  325.3 1.5 convolution_add_fusion.1
  326.8 1.7 reshape.209
  328.4 2.1 fusion.52
  330.6 1.2 copy.47
  332.9 11.6 %all_gather.15 = bf16[1536,256]{1,0:T(8,128)(2,1)} all-gather(bf16[192,256]{1,0:T(8,128)(2,1)S(1)} %copy.50), channel_id=1, replica_groups=mesh['gx'=8,'gy'=4] {'gx'}, dimensions={0}, use_global_device_ids=true | all-gather | bytes 884736 | tf_op jit(solution)/shard_map/all_gather | solution.py:121
  344.5 2.3 copy.51
  346.8 3.4 subtract_convert_fusion.1
  350.2 10.5 %fusion.53 = (f32[2,7,192]{2,1,0:T(8,128)S(1)}, f32[2,7,192,1536]{3,2,1,0:T(8,128)}) fusion(pred[192,1536]{1,0:T(8,128)(4,1)S(1)} %copy-done.19, bf16[1536,2,128,1]{0,2,3,1:T(8,128)(2,1)} %bitcast.104, bf16[192,2,7,64]{3,0,2,1:T(8,128)(2,1)} %get-tuple-element.10, bf16[192,2,7,64]{3,0,2,1:T(8,128)(2,1)} %get-tuple-element.9), kind=kOutput, calls=%fused_computation.77 | convolution fusion | flops 1074857472 | bytes 18295296 | tf_op jit(solution)/shard_map/sub | solution.py:135
  360.8 7.1 %divide_convert_fusion = bf16[2,7,192,1536]{3,2,1,0:T(8,128)(2,1)S(1)} fusion(f32[2,7,192,1536]{3,2,1,0:T(8,128)} %get-tuple-element.25, f32[2,7,192]{2,1,0:T(8,128)S(1)} %get-tuple-element.24), kind=kLoop, calls=%fused_computation.5 | loop fusion | flops 8257536 | bytes 24783360 | tf_op jit(solution)/shard_map/convert_element_type | solution.py:136
  367.9 1.5 fusion.28
  369.4 1.7 copy-done.2
  371.1 1.7 copy.77
  372.8 1.2 copy.45
  374.4 11.2 %all_gather.14 = bf16[1536,256]{1,0:T(8,128)(2,1)} all-gather(bf16[192,256]{1,0:T(8,128)(2,1)S(1)} %fusion.22), channel_id=1, replica_groups=mesh['gx'=8,'gy'=4] {'gx'}, dimensions={0}, use_global_device_ids=true | all-gather | bytes 884736 | tf_op jit(solution)/shard_map/all_gather | solution.py:122
  385.7 2.2 reshape.206
  387.9 6.6 %multiply_reduce_fusion.1 = (f32[192,2,7]{0,2,1:T(8,128)S(1)}, bf16[192,2,7,128]{3,0,2,1:T(8,128)(2,1)}) fusion(bf16[192,2,7,128]{3,2,1,0:T(8,128)(2,1)S(1)} %copy-done.7, bf16[2,7,192,1536]{3,2,1,0:T(8,128)(2,1)} %copy-done.2, bf16[1536,2,128,1]{2,1,0,3:T(2,128)(2,1)S(1)} %bitcast.98), kind=kOutput, calls=%fused_computation.25 | convolution fusion | flops 1058682240 | bytes 10430976 | tf_op jit(solution)/shard_map/kgts,skd->tkgd/dot_general | solution.py:137
  394.6 9.5 %fusion.17 = f32[192,2,7,128]{3,0,2,1:T(8,128)} fusion(bf16[1536,2,128,1]{0,2,3,1:T(8,128)(2,1)} %bitcast.105, bf16[2,7,192,1536]{3,2,1,0:T(8,128)(2,1)} %copy-done.2, f32[2,7,192]{2,1,0:T(8,128)S(1)} %bitcast.107, bf16[1536,2,128,1]{2,1,0,3:T(2,128)(2,1)S(1)} %bitcast.99, bf16[192,2,7,128]{3,2,1,0:T(8,128)(2,1)S(1)} %copy-done.7), kind=kOutput, calls=%fused_computation.22 | convolution fusion | flops 2130788352 | bytes 11905536 | tf_op jit(solution)/shard_map/kgts,skd->tkgd/dot_general | solution.py:147
  404.0 2.3 subtract_convert_fusion
  409.0 1.9 fusion.23
  412.8 1.4 fusion.24
  414.7 1.6 reshape.210
  416.3 136.6 %all-reduce.4.cloned.1.call-done = (f32[3584,64]{0,1:T(8,128)}, f32[64,1792]{1,0:T(8,128)}, f32[3584,64]{0,1:T(8,128)}, f32[64,256]{1,0:T(8,128)}) async-done(((f32[3584,64]{0,1:T(8,128)}, f32[64,1792]{1,0:T(8,128)}, f32[3584,64]{0,1:T(8,128)}, f32[64,256]{1,0:T(8,128)}), (f32[3584,64]{0,1:T(8,128)}, f32[64,1792]{1,0:T(8,128)}, f32[3584,64]{0,1:T(8,128)}, f32[64,256]{1,0:T(8,128)})) %all-reduce.4.cloned.1.call-update) | async-done | bytes 2359312 | tf_op jit(solution)/shard_map/psum | solution.py:167
  552.9 2.3 copy.105
  (84 shorter events, 12.6 us)
Async XLA Ops:
  7.2 248.6 %copy-start = (bf16[3584,448]{0,1:T(8,128)(2,1)S(1)}, bf16[3584,448]{0,1:T(8,128)(2,1)}, u32[]{:S(2)}) copy-start(bf16[3584,448]{0,1:T(8,128)(2,1)} %param.26) | copy-start | bytes 9633796
  7.2 74.7 %reduce-scatter.6.cloned.1.call-start = ((), (), s32[]{:S(2)}) async-start(), calls=%async_computation.4 | async-start | bytes 4276224 | tf_op jit(solution)/shard_map/reduce_scatter | solution.py:63
  7.2 10.2 %copy-start.9 = (bf16[4,16,1024]{2,1,0:T(8,128)(2,1)S(1)}, bf16[4,16,1024]{2,1,0:T(8,128)(2,1)}, u32[]{:S(2)}) copy-start(bf16[4,16,1024]{2,1,0:T(8,128)(2,1)} %param.18) | copy-start | bytes 393220
  29.9 92.9 %reduce-scatter.8.cloned.1.call-start = ((), (), s32[]{:S(2)}) async-start(), calls=%async_computation.5 | async-start | bytes 327680 | tf_op jit(solution)/shard_map/reduce_scatter | solution.py:72
  93.9 29.0 %copy-start.22 = (bf16[1,16,1024]{2,1,0:T(8,128)(2,1)S(1)}, bf16[1,16,1024]{2,1,0:T(8,128)(2,1)}, u32[]{:S(2)}) copy-start(bf16[1,16,1024]{2,1,0:T(8,128)(2,1)} %param.19) | copy-start | bytes 98308
  102.7 153.1 %all-gather.2.cloned.1.call-start = ((), (), s32[]{:S(2)}) async-start(), calls=%async_computation.6 | async-start | bytes 6881280 | tf_op jit(solution)/shard_map/all_gather | solution.py:90
  152.4 2.0 copy-start.23
  255.8 5.4 copy-start.4
  255.8 5.4 copy-start.14
  261.2 1.8 copy-start.15
  266.7 7.2 %copy-start.13 = (bf16[1,192,1792]{2,1,0:T(8,128)(2,1)S(1)}, bf16[1,192,1792]{2,1,0:T(8,128)(2,1)}, u32[]{:S(2)}) copy-start(bf16[1,192,1792]{2,1,0:T(8,128)(2,1)} %param.35) | copy-start | bytes 2064388
  266.7 50.3 %all-to-all-start = ((f32[4,192,576]{2,1,0:T(8,128)}), f32[4,192,576]{2,1,0:T(8,128)}, u32[]{:S(2)}, u32[]{:S(2)}) async-start(f32[4,192,576]{2,1,0:T(8,128)} %bitcast.4), calls=%async_computation.2 | async-start | bytes 3932160 | tf_op jit(solution)/shard_map/all_to_all | solution.py:99
  271.2 5.3 copy-start.3
  271.3 5.3 copy-start.16
  271.3 139.6 %reduce-scatter.10.cloned.1.call-start = ((), (), s32[]{:S(2)}) async-start(), calls=%async_computation.7 | async-start | bytes 1769472
  322.8 2.5 copy-start.10
  331.8 15.0 %copy-start.5 = (f32[192,2,7,64]{3,2,1,0:T(8,128)S(1)}, f32[192,2,7,64]{3,2,1,0:T(8,128)}, u32[]{:S(2)}) copy-start(f32[192,2,7,64]{3,2,1,0:T(8,128)} %get-tuple-element.15) | copy-start | bytes 2064388
  346.8 3.4 copy-start.19
  360.8 7.1 %copy-start.6 = (bf16[192,2,7,128]{3,2,1,0:T(8,128)(2,1)S(1)}, bf16[192,2,7,128]{3,2,1,0:T(8,128)(2,1)}, u32[]{:S(2)}) copy-start(bf16[192,2,7,128]{3,2,1,0:T(8,128)(2,1)} %reshape_squeeze.3) | copy-start | bytes 2064388
  367.9 3.2 copy-start.2
  372.7 1.5 copy-start.20
  372.8 180.1 %all-reduce.4.cloned.1.call-start = ((), (), s32[]{:S(2)}) async-start(), calls=%async_computation.8 | async-start | bytes 4718592 | tf_op jit(solution)/shard_map/psum | solution.py:167
  372.8 15.1 %copy-start.7 = (bf16[192,2,7,128]{3,2,1,0:T(8,128)(2,1)S(1)}, bf16[192,2,7,128]{3,2,1,0:T(8,128)(2,1)}, u32[]{:S(2)}) copy-start(bf16[192,2,7,128]{3,2,1,0:T(8,128)(2,1)} %reshape_squeeze.3) | copy-start | bytes 2064388
  394.6 9.5 %copy-start.18 = (f32[192,64]{1,0:T(8,128)S(1)}, f32[192,64]{1,0:T(8,128)}, u32[]{:S(2)}) copy-start(f32[192,64]{1,0:T(8,128)} %get-tuple-element.19) | copy-start | bytes 147460
  406.8 2.3 copy-start.11
  412.8 1.5 copy-start.8
  552.9 2.3 copy-start.17
  552.9 3.1 copy-start.12
  552.9 4.0 copy-start.21
  552.9 4.7 copy-start.1
Sparse Core Ops, SparseCore 0:
  30.0 51.8 reduce-scatter.5
  102.8 19.9 reduce-scatter.7
  156.0 99.6 all-gather.1
  372.9 36.5 reduce-scatter.9
  415.9 136.9 all-reduce.3
where the time goes:
time: 573 us; the launch traced here: 564 us
  waiting for transfers between devices  347 us (61%)
  matrix products  81.1 us (14%)
  blocking collectives  59 us (10%)
  local copies, waits for them, and re-layouts  35.9 us (6%)
  other arithmetic  21.5 us (4%)
  between operations  15.1 us (3%)
    psum x1, waiting for transfers between devices, on_device(): lax.psum((part_aq, part_bq, part_av, part_bv), ('gx', 'gy'))  137 us
    all_gather x1, waiting for transfers between devices, on_device(): slab_rows = lax.all_gather(normal, 'gy', axis=0, tiled=True)  99.9 us
    reduce_scatter x1, waiting for transfers between devices, on_device(): lax.psum_scatter(jnp.concatenate([gate_part, up_part], axis=1), 'gx', sca...  52 us
    all_to_all x1, waiting for transfers between devices, on_device(): lax.all_to_all(projected, 'gy', split_axis=0, concat_axis=1, tiled=True)  38.4 us
    psum x1, blocking collectives, on_device(): bridge = lax.psum(bridge_part, 'gx').astype(jnp.bfloat16)  25.4 us
    reduce_scatter x1, waiting for transfers between devices, on_device(): lax.psum_scatter(partial_out, 'gy', scatter_dimension=0, tiled=True)  20.1 us
    all_gather x1, blocking collectives, on_device(): lax.all_gather(key_local, 'gx', axis=0, tiled=True)  11.6 us
  transfers between devices with their start and end apart: 6, of which 5 were waited for; matrix products, arithmetic and copies ran while one was open for 6% of the time, Pallas kernels for 0%

commit v1 on v0

--- a/solution.py
+++ b/solution.py
@@ -165,7 +165,7 @@
     part_aq = jnp.einsum("td,tr->dr", normal, dlow_query, preferred_element_type=jnp.float32)
     part_av = jnp.einsum("td,tr->dr", normal, dlow_value, preferred_element_type=jnp.float32)
     grad_aq, grad_bq, grad_av, grad_bv = lax.psum(
-        (part_aq, part_bq, part_av, part_bv), ("gx", "gy")
+        lax.psum((part_aq, part_bq, part_av, part_bv), "gx"), "gy"
     )
     attn_out = attended.reshape(1, tokens, HEADS * HD)
     return (attn_out, grad_aq, grad_bq, grad_av, grad_bv)

time: 573 us -> 594 us (1.037)
  waiting for transfers between devices: 347 us -> 367 us
    psum x1 -> x2, waiting for transfers between devices: 137 us -> 157 us  [the longest x1 94.5 us: on_device(): lax.psum(lax.psum((part_aq, part_bq, part_av, part_bv), 'gx'), 'gy')]
  transfers between devices with their start and end apart: 6 -> 7, of which waited for: 5 -> 6; matrix products, arithmetic and copies ran while one was open for 6% -> 6% of each run, Pallas kernels for 0% -> 0%
where the time goes in v1:
time: 594 us; the launch traced here: 585 us
  waiting for transfers between devices  367 us (62%)
  matrix products  81.1 us (14%)
  blocking collectives  59.2 us (10%)
  local copies, waits for them, and re-layouts  35.7 us (6%)
  other arithmetic  21.5 us (4%)
  between operations  15.4 us (3%)
    all_gather x1, waiting for transfers between devices, on_device(): slab_rows = lax.all_gather(normal, 'gy', axis=0, tiled=True)  99.9 us
    psum x1, waiting for transfers between devices, on_device(): lax.psum(lax.psum((part_aq, part_bq, part_av, part_bv), 'gx'), 'gy')  94.5 us
    psum x1, waiting for transfers between devices, on_device(): lax.psum((part_aq, part_bq, part_av, part_bv), 'gx')  62.5 us
    reduce_scatter x1, waiting for transfers between devices, on_device(): lax.psum_scatter(jnp.concatenate([gate_part, up_part], axis=1), 'gx', sca...  52 us
    all_to_all x1, waiting for transfers between devices, on_device(): lax.all_to_all(projected, 'gy', split_axis=0, concat_axis=1, tiled=True)  38.4 us
    psum x1, blocking collectives, on_device(): bridge = lax.psum(bridge_part, 'gx').astype(jnp.bfloat16)  25.4 us
    reduce_scatter x1, waiting for transfers between devices, on_device(): lax.psum_scatter(partial_out, 'gy', scatter_dimension=0, tiled=True)  20.1 us
  transfers between devices with their start and end apart: 7, of which 6 were waited for; matrix products, arithmetic and copies ran while one was open for 6% of the time, Pallas kernels for 0%

profile of v1, /device:TPU:0, one launch (start us, length us, event | category | flops | bytes accessed | tf_op | source)
XLA Modules:
  0.0 585.2 jit_solution(6508595556607797959)
XLA Ops:
  7.2 10.2 %fusion.54 = f32[64,7392]{1,0:T(8,128)S(1)} fusion(bf16[64,1024]{1,0:T(8,128)(2,1)} %bitcast.100, bf16[1024,7392]{0,1:T(8,128)(2,1)} %param.20), kind=kOutput, calls=%fused_computation.78 | convolution fusion | flops 968884224 | bytes 17162240 | tf_op jit(solution)/shard_map/dot_general | solution.py:61
  17.4 10.0 %fusion.55 = f32[64,7392]{1,0:T(8,128)S(1)} fusion(bf16[64,1024]{1,0:T(8,128)(2,1)S(1)} %bitcast.101, bf16[1024,7392]{0,1:T(8,128)(2,1)} %param.21), kind=kOutput, calls=%fused_computation.79 | convolution fusion | flops 968884224 | bytes 17162240 | tf_op jit(solution)/shard_map/dot_general | solution.py:62
  27.4 2.5 pad_maximum_fusion
  30.0 52.0 %reduce-scatter.6.cloned.1.call-done = f32[8,14784]{1,0:T(8,128)} async-done(((f32[64,14784]{1,0:T(8,128)}), f32[8,14784]{1,0:T(8,128)}) %reduce-scatter.6.cloned.1.call-update) | async-done | bytes 473104 | tf_op jit(solution)/shard_map/reduce_scatter | solution.py:63
  81.9 1.2 fusion.32
  83.1 10.8 %all_gather.12 = bf16[64,7392]{1,0:T(8,128)(2,1)S(1)} all-gather(bf16[8,7392]{1,0:T(8,128)(2,1)S(1)} %fusion.32), channel_id=1, replica_groups=mesh['gx'=8,'gy'=4] {'gx'}, dimensions={0}, use_global_device_ids=true | all-gather | bytes 1064448 | tf_op jit(solution)/shard_map/all_gather | solution.py:68
  93.9 8.8 %fusion.56 = f32[64,1024]{1,0:T(8,128)} fusion(bf16[64,7392]{1,0:T(8,128)(2,1)S(1)} %all_gather.12, bf16[7392,1024]{1,0:T(8,128)(2,1)} %param.22), kind=kOutput, calls=%fused_computation.80 | convolution fusion | flops 968884224 | bytes 16347136 | tf_op jit(solution)/shard_map/dot_general | solution.py:67
  102.8 20.1 %reduce-scatter.8.cloned.1.call-done = f32[16,1024]{1,0:T(8,128)} async-done(((f32[64,1024]{1,0:T(8,128)}), f32[16,1024]{1,0:T(8,128)}) %reduce-scatter.8.cloned.1.call-update) | async-done | bytes 65552 | tf_op jit(solution)/shard_map/reduce_scatter | solution.py:72
  122.8 4.2 fusion.41
  127.0 25.4 %all-reduce.9 = bf16[16,3584]{1,0:T(8,128)(2,1)S(1)} all-reduce(f32[16,3584]{1,0:T(8,128)S(1)} %fusion.41), channel_id=1, replica_groups=mesh['gx'=8,'gy'=4] {'gx'}, use_global_device_ids=true, to_apply=%region_2.3 | all-reduce | flops 57344 | bytes 344064 | tf_op jit(solution)/shard_map/psum | solution.py:75
  152.4 2.0 multiply_reduce_fusion
  154.5 1.5 multiply_convert_fusion
  155.9 99.9 %all-gather.2.cloned.1.call-done = bf16[768,3584]{1,0:T(8,128)(2,1)} async-done(((bf16[192,3584]{1,0:T(8,128)(2,1)}), bf16[768,3584]{1,0:T(8,128)(2,1)}) %all-gather.2.cloned.1.call-update) | async-done | bytes 5505040 | tf_op jit(solution)/shard_map/all_gather | solution.py:90
  255.8 5.4 fusion.57
  261.2 1.8 fusion.58
  263.0 1.8 fusion.59
  264.9 1.8 copy.44
  266.7 4.6 all-to-all-start
  273.9 1.7 reshape_squeeze.3
  277.1 1.6 convolution_convert_fusion.4
  278.7 38.4 %all-to-all-done = f32[4,192,576]{2,1,0:T(8,128)} async-done(((f32[4,192,576]{2,1,0:T(8,128)}), f32[4,192,576]{2,1,0:T(8,128)}, u32[]{:S(2)}, u32[]{:S(2)}) %all-to-all-start) | async-done | bytes 1769504 | tf_op jit(solution)/shard_map/all_to_all | solution.py:99
  317.0 1.5 slice.50
  318.6 2.1 fusion.51
  320.7 2.2 copy.52
  322.9 2.5 reshape.208
  325.3 1.5 convolution_add_fusion.1
  326.8 1.7 reshape.209
  328.5 2.2 fusion.52
  333.0 11.6 %all_gather.15 = bf16[1536,256]{1,0:T(8,128)(2,1)} all-gather(bf16[192,256]{1,0:T(8,128)(2,1)S(1)} %copy.50), channel_id=1, replica_groups=mesh['gx'=8,'gy'=4] {'gx'}, dimensions={0}, use_global_device_ids=true | all-gather | bytes 884736 | tf_op jit(solution)/shard_map/all_gather | solution.py:121
  344.6 2.3 copy.51
  346.9 3.4 subtract_convert_fusion.1
  350.3 10.6 %fusion.53 = (f32[2,7,192]{2,1,0:T(8,128)S(1)}, f32[2,7,192,1536]{3,2,1,0:T(8,128)}) fusion(pred[192,1536]{1,0:T(8,128)(4,1)S(1)} %copy-done.19, bf16[1536,2,128,1]{0,2,3,1:T(8,128)(2,1)} %bitcast.104, bf16[192,2,7,64]{3,0,2,1:T(8,128)(2,1)} %get-tuple-element.14, bf16[192,2,7,64]{3,0,2,1:T(8,128)(2,1)} %get-tuple-element.13), kind=kOutput, calls=%fused_computation.77 | convolution fusion | flops 1074857472 | bytes 18295296 | tf_op jit(solution)/shard_map/sub | solution.py:135
  360.9 7.1 %divide_convert_fusion = bf16[2,7,192,1536]{3,2,1,0:T(8,128)(2,1)S(1)} fusion(f32[2,7,192,1536]{3,2,1,0:T(8,128)} %get-tuple-element.29, f32[2,7,192]{2,1,0:T(8,128)S(1)} %get-tuple-element.28), kind=kLoop, calls=%fused_computation.5 | loop fusion | flops 8257536 | bytes 24783360 | tf_op jit(solution)/shard_map/convert_element_type | solution.py:136
  367.9 1.5 fusion.28
  369.4 1.7 copy-done.2
  371.1 1.7 copy.77
  372.9 1.2 copy.45
  374.5 11.5 %all_gather.14 = bf16[1536,256]{1,0:T(8,128)(2,1)} all-gather(bf16[192,256]{1,0:T(8,128)(2,1)S(1)} %fusion.22), channel_id=1, replica_groups=mesh['gx'=8,'gy'=4] {'gx'}, dimensions={0}, use_global_device_ids=true | all-gather | bytes 884736 | tf_op jit(solution)/shard_map/all_gather | solution.py:122
  386.0 2.0 reshape.206
  388.0 6.6 %multiply_reduce_fusion.1 = (f32[192,2,7]{0,2,1:T(8,128)S(1)}, bf16[192,2,7,128]{3,0,2,1:T(8,128)(2,1)}) fusion(bf16[192,2,7,128]{3,2,1,0:T(8,128)(2,1)S(1)} %copy-done.7, bf16[2,7,192,1536]{3,2,1,0:T(8,128)(2,1)} %copy-done.2, bf16[1536,2,128,1]{2,1,0,3:T(2,128)(2,1)S(1)} %bitcast.98), kind=kOutput, calls=%fused_computation.25 | convolution fusion | flops 1058682240 | bytes 10430976 | tf_op jit(solution)/shard_map/kgts,skd->tkgd/dot_general | solution.py:137
  394.7 9.5 %fusion.17 = f32[192,2,7,128]{3,0,2,1:T(8,128)} fusion(bf16[1536,2,128,1]{0,2,3,1:T(8,128)(2,1)} %bitcast.105, bf16[2,7,192,1536]{3,2,1,0:T(8,128)(2,1)} %copy-done.2, f32[2,7,192]{2,1,0:T(8,128)S(1)} %bitcast.107, bf16[1536,2,128,1]{2,1,0,3:T(2,128)(2,1)S(1)} %bitcast.99, bf16[192,2,7,128]{3,2,1,0:T(8,128)(2,1)S(1)} %copy-done.7), kind=kOutput, calls=%fused_computation.22 | convolution fusion | flops 2130788352 | bytes 11905536 | tf_op jit(solution)/shard_map/kgts,skd->tkgd/dot_general | solution.py:147
  404.1 2.3 subtract_convert_fusion
  409.1 1.9 fusion.23
  412.9 1.4 fusion.24
  414.4 62.5 %all-reduce.6.cloned.1.call-done = (f32[3584,64]{0,1:T(8,128)}, f32[64,1792]{1,0:T(8,128)}, f32[3584,64]{0,1:T(8,128)}, f32[64,256]{1,0:T(8,128)}) async-done(((f32[3584,64]{0,1:T(8,128)}, f32[64,1792]{1,0:T(8,128)}, f32[3584,64]{0,1:T(8,128)}, f32[64,256]{1,0:T(8,128)}), (f32[3584,64]{0,1:T(8,128)}, f32[64,1792]{1,0:T(8,128)}, f32[3584,64]{0,1:T(8,128)}, f32[64,256]{1,0:T(8,128)})) %all-reduce.6.cloned.1.call-update) | async-done | bytes 2359312 | tf_op jit(solution)/shard_map/psum | solution.py:168
  477.4 1.6 reshape.210
  479.0 94.5 %all-reduce.8.cloned.1.call-done = (f32[3584,64]{0,1:T(8,128)}, f32[64,1792]{1,0:T(8,128)}, f32[3584,64]{0,1:T(8,128)}, f32[64,256]{1,0:T(8,128)}) async-done(((f32[3584,64]{0,1:T(8,128)}, f32[64,1792]{1,0:T(8,128)}, f32[3584,64]{0,1:T(8,128)}, f32[64,256]{1,0:T(8,128)}), (f32[3584,64]{0,1:T(8,128)}, f32[64,1792]{1,0:T(8,128)}, f32[3584,64]{0,1:T(8,128)}, f32[64,256]{1,0:T(8,128)})) %all-reduce.8.cloned.1.call-update) | async-done | bytes 2359312 | tf_op jit(solution)/shard_map/psum | solution.py:167
  573.5 2.3 copy.109
  (87 shorter events, 13.8 us)
Async XLA Ops:
  7.2 248.6 %copy-start = (bf16[3584,448]{0,1:T(8,128)(2,1)S(1)}, bf16[3584,448]{0,1:T(8,128)(2,1)}, u32[]{:S(2)}) copy-start(bf16[3584,448]{0,1:T(8,128)(2,1)} %param.26) | copy-start | bytes 9633796
  7.2 74.8 %reduce-scatter.6.cloned.1.call-start = ((), (), s32[]{:S(2)}) async-start(), calls=%async_computation.4 | async-start | bytes 4276224 | tf_op jit(solution)/shard_map/reduce_scatter | solution.py:63
  7.2 10.2 %copy-start.9 = (bf16[4,16,1024]{2,1,0:T(8,128)(2,1)S(1)}, bf16[4,16,1024]{2,1,0:T(8,128)(2,1)}, u32[]{:S(2)}) copy-start(bf16[4,16,1024]{2,1,0:T(8,128)(2,1)} %param.18) | copy-start | bytes 393220
  29.9 92.9 %reduce-scatter.8.cloned.1.call-start = ((), (), s32[]{:S(2)}) async-start(), calls=%async_computation.5 | async-start | bytes 327680 | tf_op jit(solution)/shard_map/reduce_scatter | solution.py:72
  93.9 29.0 %copy-start.22 = (bf16[1,16,1024]{2,1,0:T(8,128)(2,1)S(1)}, bf16[1,16,1024]{2,1,0:T(8,128)(2,1)}, u32[]{:S(2)}) copy-start(bf16[1,16,1024]{2,1,0:T(8,128)(2,1)} %param.19) | copy-start | bytes 98308
  102.7 153.1 %all-gather.2.cloned.1.call-start = ((), (), s32[]{:S(2)}) async-start(), calls=%async_computation.6 | async-start | bytes 6881280 | tf_op jit(solution)/shard_map/all_gather | solution.py:90
  152.4 2.0 copy-start.23
  255.8 5.4 copy-start.4
  255.8 5.4 copy-start.14
  261.2 1.8 copy-start.15
  266.7 7.2 %copy-start.13 = (bf16[1,192,1792]{2,1,0:T(8,128)(2,1)S(1)}, bf16[1,192,1792]{2,1,0:T(8,128)(2,1)}, u32[]{:S(2)}) copy-start(bf16[1,192,1792]{2,1,0:T(8,128)(2,1)} %param.35) | copy-start | bytes 2064388
  266.7 50.3 %all-to-all-start = ((f32[4,192,576]{2,1,0:T(8,128)}), f32[4,192,576]{2,1,0:T(8,128)}, u32[]{:S(2)}, u32[]{:S(2)}) async-start(f32[4,192,576]{2,1,0:T(8,128)} %bitcast.4), calls=%async_computation.2 | async-start | bytes 3932160 | tf_op jit(solution)/shard_map/all_to_all | solution.py:99
  271.3 5.3 copy-start.3
  271.3 5.3 copy-start.16
  271.3 139.7 %reduce-scatter.10.cloned.1.call-start = ((), (), s32[]{:S(2)}) async-start(), calls=%async_computation.7 | async-start | bytes 1769472
  322.9 2.5 copy-start.10
  331.8 15.0 %copy-start.5 = (f32[192,2,7,64]{3,2,1,0:T(8,128)S(1)}, f32[192,2,7,64]{3,2,1,0:T(8,128)}, u32[]{:S(2)}) copy-start(f32[192,2,7,64]{3,2,1,0:T(8,128)} %get-tuple-element.19) | copy-start | bytes 2064388
  346.9 3.4 copy-start.19
  360.9 7.1 %copy-start.6 = (bf16[192,2,7,128]{3,2,1,0:T(8,128)(2,1)S(1)}, bf16[192,2,7,128]{3,2,1,0:T(8,128)(2,1)}, u32[]{:S(2)}) copy-start(bf16[192,2,7,128]{3,2,1,0:T(8,128)(2,1)} %reshape_squeeze.3) | copy-start | bytes 2064388
  367.9 3.2 copy-start.2
  372.8 1.5 copy-start.20
  372.9 104.1 %all-reduce.6.cloned.1.call-start = ((), (), s32[]{:S(2)}) async-start(), calls=%async_computation.8 | async-start | bytes 4718592 | tf_op jit(solution)/shard_map/psum | solution.py:168
  372.9 15.1 %copy-start.7 = (bf16[192,2,7,128]{3,2,1,0:T(8,128)(2,1)S(1)}, bf16[192,2,7,128]{3,2,1,0:T(8,128)(2,1)}, u32[]{:S(2)}) copy-start(bf16[192,2,7,128]{3,2,1,0:T(8,128)(2,1)} %reshape_squeeze.3) | copy-start | bytes 2064388
  394.7 9.5 %copy-start.18 = (f32[192,64]{1,0:T(8,128)S(1)}, f32[192,64]{1,0:T(8,128)}, u32[]{:S(2)}) copy-start(f32[192,64]{1,0:T(8,128)} %get-tuple-element.23) | copy-start | bytes 147460
  406.9 2.3 copy-start.11
  414.3 62.6 %copy-start.8 = (bf16[192,2,7,128]{3,0,2,1:T(8,128)(2,1)S(1)}, bf16[192,2,7,128]{3,0,2,1:T(8,128)(2,1)}, u32[]{:S(2)}) copy-start(bf16[192,2,7,128]{3,0,2,1:T(8,128)(2,1)} %get-tuple-element.31) | copy-start | bytes 2064388
  414.3 159.2 %all-reduce.8.cloned.1.call-start = ((), (), s32[]{:S(2)}) async-start(), calls=%async_computation.9 | async-start | bytes 4718592 | tf_op jit(solution)/shard_map/psum | solution.py:167
  573.5 2.3 copy-start.17
  573.5 3.1 copy-start.12
  573.5 4.0 copy-start.21
  573.5 4.7 copy-start.1
Sparse Core Ops, SparseCore 0:
  30.0 51.8 reduce-scatter.5
  102.8 19.9 reduce-scatter.7
  156.1 99.6 all-gather.1
  373.0 36.4 reduce-scatter.9
  414.4 62.4 all-reduce.5
  479.4 94.0 all-reduce.7
